TPU v7x, 32 devices: a whole 2x2x4 slice. The times are simulated.
32 devices in a mesh: hour: 2 (over y), pair: 4 (over z), freq: 2 (over x), sub: 2 (over core).
Axes of the slice: x: 2, y: 2, z: 4, core: 2. Of those that a mesh axis runs over, the one named last changes fastest.
Arguments:
- raw: float32 [512, 4096], P('freq', ('hour', 'pair', 'sub')), parts along dimension 1, may hold values from -60 to 60
- offsets: int32 [16], P(('hour', 'pair', 'sub')), parts along dimension 0, may hold values from 0 to 255
- pair_mask: int32 [4, 2], P('pair'), may hold values 0 or 1
Outputs:
- correlations: bfloat16 [8, 3, 128, 128, 256], P(('hour', 'pair'), None, 'sub', 'freq'), parts along dimension 0
There are 2 independent parts, one for each index of `hour`. A program takes and returns all parts, laid end to end along the dimension named above; an argument that names none is the same for every part. Nothing has to cross between parts.
All inputs are finite; a program needn't handle non-finite values. No bound on the sum of `pair_mask` on one device may be relied on, other than what follows from the above.
Results may differ from a plain program's by a relative error of at most 0.0056.
Values may be sent and summed in bfloat16 or wider, within the bound.
No kernel may reach another device: no remote copies, remote signals or barrier semaphores. Data moves between devices by JAX's collectives and lax.ppermute only.
A program may use at most 64 MiB of HBM per device.

v0:
```python
import math
import jax
import jax.numpy as jnp
from jax import lax
from jax.sharding import PartitionSpec as P

F = 256
REACH = 2
LAGS = 256
STEP = 256


def shifted(value, axis, steps):
    count = lax.axis_size(axis)
    initial, last = (max(0, -steps), min(count, count - steps))
    return lax.ppermute(value, axis, [(source, source + steps) for source in range(initial, last)])


def dft_basis(freqs, imaginary, span):
    samples = jnp.arange(span, dtype=jnp.int32)
    phase = samples[:, None] * freqs[None, :] % span
    angle = 2.0 * math.pi / span * phase.astype(jnp.float32)
    values = jnp.where(imaginary[None, :], -jnp.sin(angle), jnp.cos(angle)) / math.sqrt(span)
    return values.astype(jnp.bfloat16)


def lag_basis(freqs, imaginary, span, lag_count, bins):
    delays = jnp.arange(lag_count, dtype=jnp.int32) - lag_count // 2
    phase = freqs[:, None] * delays[None, :] % span
    angle = 2.0 * math.pi / span * phase.astype(jnp.float32)
    values = jnp.where(imaginary[:, None], -jnp.sin(angle), jnp.cos(angle)) / math.sqrt(bins)
    return values.astype(jnp.bfloat16)


def tapered(windows):
    span = windows.shape[-1]
    centred = windows - jnp.mean(windows, axis=-1, keepdims=True)
    power = jnp.mean(centred * centred, axis=-1, keepdims=True)
    ticks = jnp.arange(span, dtype=jnp.float32)
    hann_taper = 0.5 - 0.5 * jnp.cos(2.0 * math.pi / span * ticks)
    return (centred * lax.rsqrt(power + 1e-05) * hann_taper).astype(jnp.bfloat16)


def cross_spectra(left, right, factor):
    row_count = left.shape[0]
    col_count = right.shape[0]
    bins = left.shape[3]
    turned = jnp.stack([left[:, :, 1], -left[:, :, 0]], axis=2)
    real_part = jnp.einsum("rwtf,cwtf->rcf", left, right, preferred_element_type=jnp.float32)
    imaginary_part = jnp.einsum("rwtf,cwtf->rcf", turned, right, preferred_element_type=jnp.float32)
    joined = jnp.stack([real_part, imaginary_part], axis=2)
    return joined.reshape(row_count, col_count, 2 * bins) * factor


def body(raw, offsets, pair_mask):
    span = 2 * F
    freq_count = lax.axis_size("freq")
    segment = raw.shape[1]
    extra = (span + segment - 1) // segment
    pieces = [raw]
    for ahead in range(1, extra + 1):
        pieces.append(shifted(raw, ("pair", "sub"), -ahead))
    record = jnp.concatenate(pieces, axis=1)
    starts = jnp.arange(offsets.shape[0], dtype=jnp.int32) * STEP + offsets
    windows = jax.vmap(lambda begin: lax.dynamic_slice_in_dim(record, begin, span, 1), out_axes=1)(
        starts
    )
    column = jnp.arange(span, dtype=jnp.int32)
    freqs = column % F
    imaginary = column >= F
    basis = dft_basis(freqs, imaginary, span)
    spectra = jnp.dot(tapered(windows), basis, preferred_element_type=jnp.float32).astype(
        jnp.bfloat16
    )
    spectra = spectra.reshape(spectra.shape[0], spectra.shape[1], 2, F)
    halves = lax.all_to_all(
        lax.all_to_all(spectra, "freq", split_axis=3, concat_axis=0, tiled=True),
        ("pair", "sub"),
        split_axis=0,
        concat_axis=1,
        tiled=True,
    )
    block = lax.all_gather(halves, "sub", axis=0, tiled=True)
    factor = 1.0 / halves.shape[1]
    full_block = lax.all_gather(block, "freq", axis=3, tiled=True)
    row_count = halves.shape[0]
    rows = lax.dynamic_slice_in_dim(full_block, lax.axis_index("sub") * row_count, row_count, 0)
    col_count = full_block.shape[0] // freq_count
    own_columns = lax.dynamic_slice_in_dim(
        full_block, lax.axis_index("freq") * col_count, col_count, 0
    )
    lag_table = lag_basis(freqs, imaginary, span, LAGS, F)

    def transform(partner):
        term = cross_spectra(rows, partner, factor).astype(jnp.bfloat16)
        return jnp.einsum(
            "pcf,fl->pcl", term, lag_table, preferred_element_type=jnp.float32
        ).astype(jnp.bfloat16)

    def silent(unused):
        return jnp.zeros((row_count, col_count, LAGS), jnp.bfloat16)

    outputs = [transform(own_columns)]
    for offset in range(1, REACH + 1):
        partner = shifted(own_columns, "pair", -offset)
        outputs.append(lax.cond(pair_mask[0, offset - 1] == 1, transform, silent, partner))
    result = jnp.stack(outputs)
    return result[None]


def solution(mesh):
    return jax.shard_map(
        body,
        mesh=mesh,
        in_specs=(P("freq", ("hour", "pair", "sub")), P(("hour", "pair", "sub")), P("pair", None)),
        out_specs=P(("hour", "pair"), None, "sub", "freq", None),
        check_vma=False,
    )
```

profile of v0, /device:TPU:16, one launch (start us, length us, event | category | flops | bytes accessed | tf_op | source)
XLA Modules:
  0.0 169.7 jit_solution(11203225285981303011)
XLA Ops:
  6.5 2.5 %collective-permute-start.1 = (f32[256,256]{1,0:T(8,128)}, f32[256,256]{1,0:T(8,128)S(1)}, u32[]{:S(2)}, u32[]{:S(2)}) collective-permute-start(f32[256,256]{1,0:T(8,128)} %param.7), channel_id=1, source_target_pairs={{4,0},{5,1},{8,4},{9,5},{12,8},{13,9},{6,2},{7,3},{10,6},{11,7},{1... | collective-permute-start | bytes 786440 | tf_op jit(solution)/shard_map/ppermute | solution.py:16
  9.0 1.9 %collective-permute-start = (f32[256,256]{1,0:T(8,128)}, f32[256,256]{1,0:T(8,128)S(1)}, u32[]{:S(2)}, u32[]{:S(2)}) collective-permute-start(f32[256,256]{1,0:T(8,128)} %param.7), channel_id=1, source_target_pairs={{1,0},{4,1},{5,4},{8,5},{9,8},{12,9},{13,12},{3,2},{6,3},{7,6},{10... | collective-permute-start | bytes 786440 | tf_op jit(solution)/shard_map/ppermute | solution.py:16
  11.7 5.1 %collective-permute-done.1 = f32[256,256]{1,0:T(8,128)S(1)} collective-permute-done((f32[256,256]{1,0:T(8,128)}, f32[256,256]{1,0:T(8,128)S(1)}, u32[]{:S(2)}, u32[]{:S(2)}) %collective-permute-start.1) | collective-permute-done | bytes 262176 | tf_op jit(solution)/shard_map/ppermute | solution.py:16
  17.7 1.4 fusion.57
  19.4 4.5 %convolution_convert_fusion = bf16[256,512]{1,0:T(8,128)(2,1)S(1)} fusion(s32[512]{0:T(512)S(1)} %add_select_fusion.2, pred[512]{0:T(512)(128)(4,1)S(1)} %iota_compare_fusion, f32[256,512]{1,0:T(8,128)S(1)} %get-tuple-element.49, f32[512]{0:T(512)S(1)} %multiply_subtract_fusion, f32[256]{0:T(256)S(1)} %add_rsqrt_fusion, f32[256]{0:T(256)S(1)} %broadcast_multiply_fusion), kind=kOutput, calls=%fused_computation.31 | convolution fusion | flops 139591680 | bytes 793088 | tf_op jit(solution)/shard_map/dot_general | solution.py:72
  24.5 8.6 %all_to_all.36 = bf16[256,1,2,256]{0,2,1,3:T(2,128)(2,1)S(1)} all-to-all(bf16[256,1,2,256]{0,2,1,3:T(2,128)(2,1)S(1)} %copy.29), channel_id=1, replica_groups=mesh['hour'=2,'pair'=4,'freq'=2,'sub'=2] {'freq'}, dimensions={3} | all-to-all | bytes 524288 | tf_op jit(solution)/shard_map/all_to_all | solution.py:77
  33.5 10.5 %all_to_all.37 = bf16[512,1,2,128]{3,2,1,0:T(2,128)(2,1)S(1)} all-to-all(bf16[512,1,2,128]{3,2,1,0:T(2,128)(2,1)S(1)} %copy.32), channel_id=1, replica_groups=mesh['hour'=2,'pair'=4,'freq'=2,'sub'=2] {'pair','sub'}, dimensions={0} | all-to-all | bytes 524288 | tf_op jit(solution)/shard_map/all_to_all | solution.py:76
  44.1 2.3 %all-gather = bf16[128,8,1,2,128]{4,0,1,3,2:T(8,128)(2,1)} all-gather(bf16[64,8,1,2,128]{4,0,1,3,2:T(8,128)(2,1)S(1)} %bitcast.102), channel_id=2, replica_groups=mesh['hour'=2,'pair'=4,'freq'=2,'sub'=2] {'sub'}, dimensions={0}, use_global_device_ids=true | all-gather | bytes 786432 | tf_op jit(solution)/shard_map/all_gather | solution.py:83
  48.5 2.6 %multiply_convert_fusion.2 = bf16[512,256]{1,0:T(8,128)(2,1)S(1)} fusion(s32[256]{0:T(256)S(1)} %iota_add_fusion, s32[512]{0:T(512)S(1)} %add_select_fusion.2, pred[512]{0:T(512)(128)(4,1)S(1)} %iota_compare_fusion), kind=kLoop, calls=%fused_computation.61 | loop fusion | flops 2359296 | bytes 265728 | tf_op jit(solution)/shard_map/convert_element_type | solution.py:32
  51.1 17.5 %all-gather.4.cloned.1.call-done = bf16[128,8,1,2,256]{4,0,1,3,2:T(8,128)(2,1)} async-done(((bf16[128,8,1,2,128]{4,0,1,3,2:T(8,128)(2,1)}), bf16[128,8,1,2,256]{4,0,1,3,2:T(8,128)(2,1)}) %all-gather.4.cloned.1.call-update) | async-done | bytes 1048592 | tf_op jit(solution)/shard_map/all_gather | solution.py:85
  71.0 2.4 %collective-permute-start.3 = (bf16[64,8,2,256]{3,1,2,0:T(8,128)(2,1)}, bf16[64,8,2,256]{3,1,2,0:T(8,128)(2,1)S(1)}, u32[]{:S(2)}, u32[]{:S(2)}) collective-permute-start(bf16[64,8,2,256]{3,1,2,0:T(8,128)(2,1)} %copy.37), channel_id=1, source_target_pairs={{8,0},{12,4},{9,1},{13,5},{10,2},{14,6},{11,3},{15,7},{24,16},{28,... | collective-permute-start | bytes 1572872 | tf_op jit(solution)/shard_map/ppermute | solution.py:16
  73.5 2.1 %collective-permute-start.2 = (bf16[64,8,2,256]{3,1,2,0:T(8,128)(2,1)}, bf16[64,8,2,256]{3,1,2,0:T(8,128)(2,1)}, u32[]{:S(2)}, u32[]{:S(2)}) collective-permute-start(bf16[64,8,2,256]{3,1,2,0:T(8,128)(2,1)} %copy.37), channel_id=1, source_target_pairs={{4,0},{8,4},{12,8},{5,1},{9,5},{13,9},{6,2},{10,6},{14,10},{7,3},{... | collective-permute-start | bytes 1572872 | tf_op jit(solution)/shard_map/ppermute | solution.py:16
  77.6 1.4 convolution_bitcast_fusion.5
  79.0 1.4 convolution_bitcast_fusion.4
  80.4 4.6 %fusion.12 = bf16[64,64,2,256]{0,1,3,2:T(8,128)(2,1)} fusion(f32[64,64,1,256]{0,1,3,2:T(8,128)S(1)} %convolution_bitcast_fusion.4, f32[64,64,1,256]{0,1,3,2:T(8,128)S(1)} %convolution_bitcast_fusion.5), kind=kLoop, calls=%fused_computation.23 | loop fusion | flops 6291456 | bytes 12582912 | tf_op jit(solution)/shard_map/convert_element_type | solution.py:95
  85.0 12.0 %copy.36 = bf16[64,64,512]{2,1,0:T(8,128)(2,1)} copy(bf16[64,64,512]{0,1,2:T(8,128)(2,1)} %bitcast.98) | data formatting | bytes 8388608 | tf_op jit(solution)/shard_map/convert_element_type | solution.py:95
  97.0 7.0 %convert_bitcast_fusion.2 = bf16[1,64,64,256]{3,2,1,0:T(8,128)(2,1)} fusion(bf16[64,64,512]{2,1,0:T(8,128)(2,1)} %copy.36, s32[256]{0:T(256)S(1)} %iota_add_fusion, s32[512]{0:T(512)S(1)} %add_select_fusion.2, pred[512]{0:T(512)(128)(4,1)S(1)} %iota_compare_fusion), kind=kOutput, calls=%fused_computation.27 | convolution fusion | flops 1077149696 | bytes 6295040 | tf_op jit(solution)/shard_map/pcf,fl->pcl/dot_general | solution.py:96
  104.0 24.2 %conditional.3 = (bf16[1,64,64,256]{3,2,1,0:T(8,128)(2,1)S(1)}) conditional(s32[]{:T(128)} %bitcast.42, () %tuple.23, (bf16[64,8,2,256]{3,1,2,0:T(8,128)(2,1)S(1)}, bf16[64,8,2,256]{0,1,2,3:T(8,128)(2,1)S(1)}, bf16[512,256]{1,0:T(8,128)(2,1)S(1)}) %tuple.44), branch_computations={%region_4.5_spmd, %region_5.6_spmd} | conditional | flops 1148583936 | bytes 40108040 | solution.py:106
  105.4 1.4 convolution_bitcast_fusion.2
  106.8 1.4 convolution_bitcast_fusion.3
  108.2 4.6 %fusion.6 = bf16[64,64,2,256]{0,1,3,2:T(8,128)(2,1)} fusion(f32[64,64,1,256]{0,1,3,2:T(8,128)S(1)} %convolution_bitcast_fusion.2, f32[64,64,1,256]{0,1,3,2:T(8,128)S(1)} %convolution_bitcast_fusion.3), kind=kLoop, calls=%fused_computation.12 | loop fusion | flops 6291456 | bytes 12582912 | tf_op jit(solution)/shard_map/cond/branch_1_fun/convert_element_type | solution.py:95
  112.8 12.0 %copy.28 = bf16[64,64,512]{2,1,0:T(8,128)(2,1)} copy(bf16[64,64,512]{0,1,2:T(8,128)(2,1)} %bitcast.99) | data formatting | bytes 8388608 | tf_op jit(solution)/shard_map/cond/branch_1_fun/convert_element_type | solution.py:95
  124.8 3.4 %convert_bitcast_fusion.1 = bf16[1,64,64,256]{3,2,1,0:T(8,128)(2,1)S(1)} fusion(bf16[64,64,512]{2,1,0:T(8,128)(2,1)} %copy.28, bf16[512,256]{1,0:T(8,128)(2,1)S(1)} %get-tuple-element.30), kind=kOutput, calls=%fused_computation.15 | convolution fusion | flops 1074790400 | bytes 6553600 | tf_op jit(solution)/shard_map/cond/branch_1_fun/pcf,fl->pcl/dot_general | solution.py:96
  128.2 1.3 copy-done
  129.6 26.9 %conditional.2 = (bf16[1,64,64,256]{3,2,1,0:T(8,128)(2,1)}) conditional(s32[]{:T(128)} %bitcast.40, () %tuple.21, (bf16[64,8,2,256]{3,1,2,0:T(8,128)(2,1)}, bf16[64,8,2,256]{0,1,2,3:T(8,128)(2,1)S(1)}, bf16[512,256]{1,0:T(8,128)(2,1)S(1)}) %tuple.45), branch_computations={%region_2.3_spmd, %region_3.4_spmd} | conditional | flops 1148583936 | bytes 40108040 | solution.py:106
  129.6 2.6 %copy.38 = bf16[64,8,2,256]{0,1,2,3:T(8,128)(2,1)S(1)} copy(bf16[64,8,2,256]{3,1,2,0:T(8,128)(2,1)} %get-tuple-element.42) | data formatting | bytes 1048576 | tf_op jit(solution)/shard_map
  132.3 1.4 convolution_bitcast_fusion
  133.7 1.4 convolution_bitcast_fusion.1
  135.1 4.6 %fusion = bf16[64,64,2,256]{0,1,3,2:T(8,128)(2,1)} fusion(f32[64,64,1,256]{0,1,3,2:T(8,128)S(1)} %convolution_bitcast_fusion, f32[64,64,1,256]{0,1,3,2:T(8,128)S(1)} %convolution_bitcast_fusion.1), kind=kLoop, calls=%fused_computation.1 | loop fusion | flops 6291456 | bytes 12582912 | tf_op jit(solution)/shard_map/cond/branch_1_fun/convert_element_type | solution.py:95
  139.7 12.0 %copy.26 = bf16[64,64,512]{2,1,0:T(8,128)(2,1)} copy(bf16[64,64,512]{0,1,2:T(8,128)(2,1)} %bitcast.100) | data formatting | bytes 8388608 | tf_op jit(solution)/shard_map/cond/branch_1_fun/convert_element_type | solution.py:95
  151.7 4.8 %convert_bitcast_fusion = bf16[1,64,64,256]{3,2,1,0:T(8,128)(2,1)} fusion(bf16[64,64,512]{2,1,0:T(8,128)(2,1)} %copy.26, bf16[512,256]{1,0:T(8,128)(2,1)S(1)} %get-tuple-element.27), kind=kOutput, calls=%fused_computation.4 | convolution fusion | flops 1074790400 | bytes 6553600 | tf_op jit(solution)/shard_map/cond/branch_1_fun/pcf,fl->pcl/dot_general | solution.py:96
  156.5 6.4 %maximum_bitcast_fusion = bf16[1,3,64,64,256]{4,3,2,1,0:T(8,128)(2,1)} fusion(bf16[1,64,64,256]{3,2,1,0:T(8,128)(2,1)} %copy-done, bf16[1,64,64,256]{3,2,1,0:T(8,128)(2,1)} %get-tuple-element.60, bf16[1,64,64,256]{3,2,1,0:T(8,128)(2,1)} %convert_bitcast_fusion.2), kind=kLoop, calls=%fused_computation.24 | loop fusion | flops 6291456 | bytes 12582912 | tf_op jit(solution)/shard_map/broadcast_in_dim | solution.py:108
  (30 shorter events, 8.9 us)
Async XLA Ops:
  6.5 39.9 %copy-start.1 = (s32[1,2]{1,0:T(1,128)S(1)}, s32[1,2]{1,0:T(1,128)}, u32[]{:S(2)}) copy-start(s32[1,2]{1,0:T(1,128)} %param.9) | copy-start | bytes 28
  6.5 62.1 %all-gather.4.cloned.1.call-start = ((), (), s32[]{:S(2)}) async-start(), calls=%async_computation.2 | async-start | bytes 1572864 | tf_op jit(solution)/shard_map/all_gather | solution.py:85
  6.5 10.3 %collective-permute-start.1 = (f32[256,256]{1,0:T(8,128)}, f32[256,256]{1,0:T(8,128)S(1)}, u32[]{:S(2)}, u32[]{:S(2)}) collective-permute-start(f32[256,256]{1,0:T(8,128)} %param.7), channel_id=1, source_target_pairs={{4,0},{5,1},{8,4},{9,5},{12,8},{13,9},{6,2},{7,3},{10,6},{11,7},{1... | collective-permute-start | bytes 786440 | tf_op jit(solution)/shard_map/ppermute | solution.py:16
  9.0 8.7 %collective-permute-start = (f32[256,256]{1,0:T(8,128)}, f32[256,256]{1,0:T(8,128)S(1)}, u32[]{:S(2)}, u32[]{:S(2)}) collective-permute-start(f32[256,256]{1,0:T(8,128)} %param.7), channel_id=1, source_target_pairs={{1,0},{4,1},{5,4},{8,5},{9,8},{12,9},{13,12},{3,2},{6,3},{7,6},{10... | collective-permute-start | bytes 786440 | tf_op jit(solution)/shard_map/ppermute | solution.py:16
  71.0 33.0 %collective-permute-start.3 = (bf16[64,8,2,256]{3,1,2,0:T(8,128)(2,1)}, bf16[64,8,2,256]{3,1,2,0:T(8,128)(2,1)S(1)}, u32[]{:S(2)}, u32[]{:S(2)}) collective-permute-start(bf16[64,8,2,256]{3,1,2,0:T(8,128)(2,1)} %copy.37), channel_id=1, source_target_pairs={{8,0},{12,4},{9,1},{13,5},{10,2},{14,6},{11,3},{15,7},{24,16},{28,... | collective-permute-start | bytes 1572872 | tf_op jit(solution)/shard_map/ppermute | solution.py:16
  73.5 54.8 %collective-permute-start.2 = (bf16[64,8,2,256]{3,1,2,0:T(8,128)(2,1)}, bf16[64,8,2,256]{3,1,2,0:T(8,128)(2,1)}, u32[]{:S(2)}, u32[]{:S(2)}) collective-permute-start(bf16[64,8,2,256]{3,1,2,0:T(8,128)(2,1)} %copy.37), channel_id=1, source_target_pairs={{4,0},{8,4},{12,8},{5,1},{9,5},{13,9},{6,2},{10,6},{14,10},{7,3},{... | collective-permute-start | bytes 1572872 | tf_op jit(solution)/shard_map/ppermute | solution.py:16
  128.2 1.3 copy-start
Sparse Core Ops, SparseCore 0:
  46.6 22.0 all-gather.3
where the time goes:
time: 171 us; the launch traced here: 170 us
  local copies, waits for them, and re-layouts  47.2 us (28%)
  matrix products  27.9 us (16%)
  other arithmetic  25 us (15%)
  waiting for transfers between devices  23.5 us (14%)
  blocking collectives  21.4 us (13%)
  between operations  15.6 us (9%)
  starting transfers between devices  8.95 us (5%)
    convert_element_type x3, local copies, waits for them, and re-layouts, transform(): term = cross_spectra(rows, partner, factor).astype(jnp.bfloat16)  35.9 us
    all_gather x1, waiting for transfers between devices, body(): full_block = lax.all_gather(block, 'freq', axis=3, tiled=True)  17.5 us
    dot_general x3, matrix products, transform(): jnp.einsum('pcf,fl->pcl', term, lag_table, preferred_element_type=jnp.flo...  15.2 us
    convert_element_type x3, other arithmetic, transform(): term = cross_spectra(rows, partner, factor).astype(jnp.bfloat16)  13.9 us
    all_to_all x1, blocking collectives, body(): lax.all_to_all(lax.all_to_all(spectra, 'freq', split_axis=3, concat_axis=...  10.5 us
    ppermute x4, starting transfers between devices, shifted(): lax.ppermute(value, axis, [(source, source + steps) for source in range(i...  8.95 us
    all_to_all x1, blocking collectives, body(): lax.all_to_all(spectra, 'freq', split_axis=3, concat_axis=0, tiled=True)  8.58 us
    broadcast_in_dim x1, other arithmetic, body(): return result[None]  6.38 us
  transfers between devices with their start and end apart: 5, of which 3 were waited for; matrix products, arithmetic and copies ran while one was open for 33% of the time, Pallas kernels for 0%

commit v1 on v0

--- a/solution.py
+++ b/solution.py
@@ -82,7 +82,17 @@
     )
     block = lax.all_gather(halves, "sub", axis=0, tiled=True)
     factor = 1.0 / halves.shape[1]
-    full_block = lax.all_gather(block, "freq", axis=3, tiled=True)
+    arr_out, a_next = (lax.psum(1, "freq"), lax.axis_index("freq"))
+    full_block, v_now = (block, 1)
+    while v_now < arr_out:
+        by_rank = []
+        for j in range(arr_out):
+            by_rank.append((j, j ^ v_now))
+        big = lax.ppermute(full_block, "freq", by_rank)
+        opened = jnp.concatenate([full_block, big], 3)
+        everything = jnp.concatenate([big, full_block], 3)
+        full_block = jnp.where(a_next & v_now == 0, opened, everything)
+        v_now = 2 * v_now
     row_count = halves.shape[0]
     rows = lax.dynamic_slice_in_dim(full_block, lax.axis_index("sub") * row_count, row_count, 0)
     col_count = full_block.shape[0] // freq_count

time: 171 us -> 157 us (0.918)
  between operations: 15.6 us -> 2.11 us
  waiting for transfers between devices: 23.5 us -> 18 us
  starting transfers between devices: 8.95 us -> 11.8 us
    all_gather x1 -> x0, waiting for transfers between devices: 17.5 us -> none  [body(): full_block = lax.all_gather(block, 'freq', axis=3, tiled=True)]
    ppermute x0 -> x1, waiting for transfers between devices: none -> 9.36 us  [body(): big = lax.ppermute(full_block, 'freq', by_rank)]
    ppermute x4, starting transfers between devices: 8.95 us -> 11.7 us  [shifted(): lax.ppermute(value, axis, [(source, source + steps) for source in range(i...]
    ppermute x4, waiting for transfers between devices: 6.02 us -> 8.64 us  [shifted(): lax.ppermute(value, axis, [(source, source + steps) for source in range(i...]
  transfers between devices with their start and end apart: 5 -> 5, of which waited for: 3 -> 3; matrix products, arithmetic and copies ran while one was open for 33% -> 36% of each run, Pallas kernels for 0% -> 0%
where the time goes in v1:
time: 157 us; the launch traced here: 156 us
  local copies, waits for them, and re-layouts  47.8 us (30%)
  matrix products  29.1 us (19%)
  other arithmetic  26.3 us (17%)
  blocking collectives  20.3 us (13%)
  waiting for transfers between devices  18 us (11%)
  starting transfers between devices  11.8 us (8%)
  between operations  2.11 us (1%)
    convert_element_type x3, local copies, waits for them, and re-layouts, transform(): term = cross_spectra(rows, partner, factor).astype(jnp.bfloat16)  35.9 us
    dot_general x3, matrix products, transform(): jnp.einsum('pcf,fl->pcl', term, lag_table, preferred_element_type=jnp.flo...  15.2 us
    convert_element_type x3, other arithmetic, transform(): term = cross_spectra(rows, partner, factor).astype(jnp.bfloat16)  13.8 us
    ppermute x4, starting transfers between devices, shifted(): lax.ppermute(value, axis, [(source, source + steps) for source in range(i...  11.7 us
    all_to_all x1, blocking collectives, body(): lax.all_to_all(lax.all_to_all(spectra, 'freq', split_axis=3, concat_axis=...  10.4 us
    ppermute x1, waiting for transfers between devices, body(): big = lax.ppermute(full_block, 'freq', by_rank)  9.36 us
    ppermute x4, waiting for transfers between devices, shifted(): lax.ppermute(value, axis, [(source, source + steps) for source in range(i...  8.64 us
    all_to_all x1, blocking collectives, body(): lax.all_to_all(spectra, 'freq', split_axis=3, concat_axis=0, tiled=True)  7.73 us
  transfers between devices with their start and end apart: 5, of which 3 were waited for; matrix products, arithmetic and copies ran while one was open for 36% of the time, Pallas kernels for 0%

profile of v1, /device:TPU:16, one launch (start us, length us, event | category | flops | bytes accessed | tf_op | source)
XLA Modules:
  0.0 155.5 jit_solution(10606547645614035090)
XLA Ops:
  0.0 2.0 %collective-permute-start = (f32[256,256]{1,0:T(8,128)}, f32[256,256]{1,0:T(8,128)S(1)}, u32[]{:S(2)}, u32[]{:S(2)}) collective-permute-start(f32[256,256]{1,0:T(8,128)} %param.7), channel_id=1, source_target_pairs={{1,0},{4,1},{5,4},{8,5},{9,8},{12,9},{13,12},{3,2},{6,3},{7,6},{10... | collective-permute-start | bytes 786440 | tf_op jit(solution)/shard_map/ppermute | solution.py:16
  2.1 2.4 %collective-permute-start.1 = (f32[256,256]{1,0:T(8,128)}, f32[256,256]{1,0:T(8,128)S(1)}, u32[]{:S(2)}, u32[]{:S(2)}) collective-permute-start(f32[256,256]{1,0:T(8,128)} %param.7), channel_id=1, source_target_pairs={{4,0},{5,1},{8,4},{9,5},{12,8},{13,9},{6,2},{7,3},{10,6},{11,7},{1... | collective-permute-start | bytes 786440 | tf_op jit(solution)/shard_map/ppermute | solution.py:16
  5.1 2.0 %collective-permute-done = f32[256,256]{1,0:T(8,128)S(1)} collective-permute-done((f32[256,256]{1,0:T(8,128)}, f32[256,256]{1,0:T(8,128)S(1)}, u32[]{:S(2)}, u32[]{:S(2)}) %collective-permute-start) | collective-permute-done | bytes 262176 | tf_op jit(solution)/shard_map/ppermute | solution.py:16
  7.1 6.6 %collective-permute-done.1 = f32[256,256]{1,0:T(8,128)S(1)} collective-permute-done((f32[256,256]{1,0:T(8,128)}, f32[256,256]{1,0:T(8,128)S(1)}, u32[]{:S(2)}, u32[]{:S(2)}) %collective-permute-start.1) | collective-permute-done | bytes 262176 | tf_op jit(solution)/shard_map/ppermute | solution.py:16
  13.8 1.4 fusion.54
  15.5 4.5 %convolution_convert_fusion = bf16[256,512]{1,0:T(8,128)(2,1)S(1)} fusion(s32[512]{0:T(512)S(1)} %add_select_fusion.2, pred[512]{0:T(512)(128)(4,1)S(1)} %iota_compare_fusion, f32[256,512]{1,0:T(8,128)S(1)} %get-tuple-element.55, f32[512]{0:T(512)S(1)} %multiply_subtract_fusion, f32[256]{0:T(256)S(1)} %add_rsqrt_fusion, f32[256]{0:T(256)S(1)} %broadcast_multiply_fusion), kind=kOutput, calls=%fused_computation.31 | convolution fusion | flops 139591680 | bytes 793088 | tf_op jit(solution)/shard_map/dot_general | solution.py:72
  20.5 7.7 %all_to_all.36 = bf16[256,1,2,256]{0,2,1,3:T(2,128)(2,1)S(1)} all-to-all(bf16[256,1,2,256]{0,2,1,3:T(2,128)(2,1)S(1)} %copy.35), channel_id=1, replica_groups=mesh['hour'=2,'pair'=4,'freq'=2,'sub'=2] {'freq'}, dimensions={3} | all-to-all | bytes 524288 | tf_op jit(solution)/shard_map/all_to_all | solution.py:77
  28.6 10.4 %all_to_all.37 = bf16[512,1,2,128]{3,2,1,0:T(2,128)(2,1)S(1)} all-to-all(bf16[512,1,2,128]{3,2,1,0:T(2,128)(2,1)S(1)} %bitcast.95), channel_id=1, replica_groups=mesh['hour'=2,'pair'=4,'freq'=2,'sub'=2] {'pair','sub'}, dimensions={0} | all-to-all | bytes 524288 | tf_op jit(solution)/shard_map/all_to_all | solution.py:76
  39.2 2.2 %all-gather = bf16[128,8,1,2,128]{4,1,3,2,0:T(8,128)(2,1)S(1)} all-gather(bf16[64,8,1,2,128]{4,1,3,2,0:T(8,128)(2,1)S(1)} %copy.38), channel_id=2, replica_groups=mesh['hour'=2,'pair'=4,'freq'=2,'sub'=2] {'sub'}, dimensions={0}, use_global_device_ids=true | all-gather | bytes 786432 | tf_op jit(solution)/shard_map/all_gather | solution.py:83
  44.2 2.6 %multiply_convert_fusion.2 = bf16[512,256]{1,0:T(8,128)(2,1)S(1)} fusion(s32[256]{0:T(256)S(1)} %iota_add_fusion, s32[512]{0:T(512)S(1)} %add_select_fusion.2, pred[512]{0:T(512)(128)(4,1)S(1)} %iota_compare_fusion), kind=kLoop, calls=%fused_computation.60 | loop fusion | flops 2359296 | bytes 265728 | tf_op jit(solution)/shard_map/convert_element_type | solution.py:32
  46.8 9.4 %collective-permute-done.2 = bf16[128,8,2,128]{0,1,2,3:T(8,128)(2,1)S(1)} collective-permute-done((bf16[128,8,2,128]{0,1,2,3:T(8,128)(2,1)S(1)}, bf16[128,8,2,128]{0,1,2,3:T(8,128)(2,1)S(1)}, u32[]{:S(2)}, u32[]{:S(2)}) %collective-permute-start.2) | collective-permute-done | bytes 524320 | tf_op jit(solution)/shard_map/ppermute | solution.py:91
  57.0 2.2 %copy.41 = bf16[64,8,2,256]{3,1,2,0:T(8,128)(2,1)} copy(bf16[64,8,2,256]{0,1,2,3:T(8,128)(2,1)S(1)} %get-tuple-element.63) | data formatting | bytes 1048576 | tf_op jit(solution)/shard_map/dynamic_slice | solution.py:99
  59.2 3.8 %collective-permute-start.3 = (bf16[64,8,2,256]{3,1,2,0:T(8,128)(2,1)}, bf16[64,8,2,256]{3,1,2,0:T(8,128)(2,1)}, u32[]{:S(2)}, u32[]{:S(2)}) collective-permute-start(bf16[64,8,2,256]{3,1,2,0:T(8,128)(2,1)} %copy.41), channel_id=1, source_target_pairs={{4,0},{8,4},{12,8},{5,1},{9,5},{13,9},{6,2},{10,6},{14,10},{7,3},{... | collective-permute-start | bytes 1572872 | tf_op jit(solution)/shard_map/ppermute | solution.py:16
  63.0 3.5 %collective-permute-start.4 = (bf16[64,8,2,256]{3,1,2,0:T(8,128)(2,1)}, bf16[64,8,2,256]{3,1,2,0:T(8,128)(2,1)}, u32[]{:S(2)}, u32[]{:S(2)}) collective-permute-start(bf16[64,8,2,256]{3,1,2,0:T(8,128)(2,1)} %copy.41), channel_id=1, source_target_pairs={{8,0},{12,4},{9,1},{13,5},{10,2},{14,6},{11,3},{15,7},{24,16},{28,... | collective-permute-start | bytes 1572872 | tf_op jit(solution)/shard_map/ppermute | solution.py:16
  66.5 1.4 convolution_bitcast_fusion.5
  68.2 1.4 convolution_bitcast_fusion.4
  69.6 4.6 %fusion.12 = bf16[64,64,2,256]{0,1,3,2:T(8,128)(2,1)} fusion(f32[64,64,1,256]{0,1,3,2:T(8,128)S(1)} %convolution_bitcast_fusion.4, f32[64,64,1,256]{0,1,3,2:T(8,128)S(1)} %convolution_bitcast_fusion.5), kind=kLoop, calls=%fused_computation.23 | loop fusion | flops 6291456 | bytes 12582912 | tf_op jit(solution)/shard_map/convert_element_type | solution.py:105
  74.2 12.0 %copy.40 = bf16[64,64,512]{2,1,0:T(8,128)(2,1)} copy(bf16[64,64,512]{0,1,2:T(8,128)(2,1)} %bitcast.89) | data formatting | bytes 8388608 | tf_op jit(solution)/shard_map/convert_element_type | solution.py:105
  86.2 7.0 %convert_bitcast_fusion.2 = bf16[1,64,64,256]{3,2,1,0:T(8,128)(2,1)} fusion(bf16[64,64,512]{2,1,0:T(8,128)(2,1)} %copy.40, s32[256]{0:T(256)S(1)} %iota_add_fusion, s32[512]{0:T(512)S(1)} %add_select_fusion.2, pred[512]{0:T(512)(128)(4,1)S(1)} %iota_compare_fusion), kind=kOutput, calls=%fused_computation.27 | convolution fusion | flops 1077149696 | bytes 6295040 | tf_op jit(solution)/shard_map/pcf,fl->pcl/dot_general | solution.py:106
  93.2 25.6 %conditional.2 = (bf16[1,64,64,256]{3,2,1,0:T(8,128)(2,1)S(1)}) conditional(s32[]{:T(128)} %bitcast.39, () %tuple.21, (bf16[64,8,2,256]{3,1,2,0:T(8,128)(2,1)}, bf16[64,8,2,256]{0,1,2,3:T(8,128)(2,1)S(1)}, bf16[512,256]{1,0:T(8,128)(2,1)S(1)}) %tuple.22), branch_computations={%region_2.3_spmd, %region_3.4_spmd} | conditional | flops 1148583936 | bytes 40108040 | solution.py:116
  93.3 2.6 %copy.42 = bf16[64,8,2,256]{0,1,2,3:T(8,128)(2,1)S(1)} copy(bf16[64,8,2,256]{3,1,2,0:T(8,128)(2,1)} %get-tuple-element.48) | data formatting | bytes 1048576 | tf_op jit(solution)/shard_map
  97.3 1.4 convolution_bitcast_fusion.1
  98.7 4.6 %fusion = bf16[64,64,2,256]{0,1,3,2:T(8,128)(2,1)} fusion(f32[64,64,1,256]{0,1,3,2:T(8,128)S(1)} %convolution_bitcast_fusion, f32[64,64,1,256]{0,1,3,2:T(8,128)S(1)} %convolution_bitcast_fusion.1), kind=kLoop, calls=%fused_computation.1 | loop fusion | flops 6291456 | bytes 12582912 | tf_op jit(solution)/shard_map/cond/branch_1_fun/convert_element_type | solution.py:105
  103.3 12.0 %copy.32 = bf16[64,64,512]{2,1,0:T(8,128)(2,1)} copy(bf16[64,64,512]{0,1,2:T(8,128)(2,1)} %bitcast.90) | data formatting | bytes 8388608 | tf_op jit(solution)/shard_map/cond/branch_1_fun/convert_element_type | solution.py:105
  115.3 3.4 %convert_bitcast_fusion = bf16[1,64,64,256]{3,2,1,0:T(8,128)(2,1)S(1)} fusion(bf16[64,64,512]{2,1,0:T(8,128)(2,1)} %copy.32, bf16[512,256]{1,0:T(8,128)(2,1)S(1)} %get-tuple-element.27), kind=kOutput, calls=%fused_computation.4 | convolution fusion | flops 1074790400 | bytes 6553600 | tf_op jit(solution)/shard_map/cond/branch_1_fun/pcf,fl->pcl/dot_general | solution.py:106
  120.1 29.1 %conditional.3 = (bf16[1,64,64,256]{3,2,1,0:T(8,128)(2,1)}) conditional(s32[]{:T(128)} %bitcast.40, () %tuple.23, (bf16[64,8,2,256]{3,1,2,0:T(8,128)(2,1)}, bf16[64,8,2,256]{0,1,2,3:T(8,128)(2,1)S(1)}, bf16[512,256]{1,0:T(8,128)(2,1)S(1)}) %tuple.24), branch_computations={%region_4.5_spmd, %region_5.6_spmd} | conditional | flops 1148583936 | bytes 40108040 | solution.py:116
  121.2 2.6 %copy.44 = bf16[64,8,2,256]{0,1,2,3:T(8,128)(2,1)S(1)} copy(bf16[64,8,2,256]{3,1,2,0:T(8,128)(2,1)} %get-tuple-element.51) | data formatting | bytes 1048576 | tf_op jit(solution)/shard_map
  123.8 2.6 %convolution_bitcast_fusion.2 = f32[64,64,1,256]{0,1,3,2:T(8,128)S(1)} fusion(bf16[64,8,2,256]{0,1,2,3:T(8,128)(2,1)S(1)} %copy.44, bf16[64,8,1,256]{0,1,2,3:T(8,128)(2,1)} %get-tuple-element.59, bf16[64,8,1,256]{0,1,2,3:T(8,128)(2,1)} %get-tuple-element.58), kind=kOutput, calls=%fused_computation.13 | convolution fusion | flops 33816576 | bytes 5242880 | tf_op jit(solution)/shard_map/cond/branch_1_fun/rwtf,cwtf->rcf/dot_general | solution.py:50
  127.8 4.6 %fusion.6 = bf16[64,64,2,256]{0,1,3,2:T(8,128)(2,1)} fusion(f32[64,64,1,256]{0,1,3,2:T(8,128)S(1)} %convolution_bitcast_fusion.2, f32[64,64,1,256]{0,1,3,2:T(8,128)S(1)} %convolution_bitcast_fusion.3), kind=kLoop, calls=%fused_computation.12 | loop fusion | flops 6291456 | bytes 12582912 | tf_op jit(solution)/shard_map/cond/branch_1_fun/convert_element_type | solution.py:105
  132.4 12.0 %copy.34 = bf16[64,64,512]{2,1,0:T(8,128)(2,1)} copy(bf16[64,64,512]{0,1,2:T(8,128)(2,1)} %bitcast.91) | data formatting | bytes 8388608 | tf_op jit(solution)/shard_map/cond/branch_1_fun/convert_element_type | solution.py:105
  144.4 4.8 %convert_bitcast_fusion.1 = bf16[1,64,64,256]{3,2,1,0:T(8,128)(2,1)} fusion(bf16[64,64,512]{2,1,0:T(8,128)(2,1)} %copy.34, bf16[512,256]{1,0:T(8,128)(2,1)S(1)} %get-tuple-element.30), kind=kOutput, calls=%fused_computation.15 | convolution fusion | flops 1074790400 | bytes 6553600 | tf_op jit(solution)/shard_map/cond/branch_1_fun/pcf,fl->pcl/dot_general | solution.py:106
  149.1 6.4 %maximum_bitcast_fusion = bf16[1,3,64,64,256]{4,3,2,1,0:T(8,128)(2,1)} fusion(bf16[1,64,64,256]{3,2,1,0:T(8,128)(2,1)} %get-tuple-element.67, bf16[1,64,64,256]{3,2,1,0:T(8,128)(2,1)} %copy-done, bf16[1,64,64,256]{3,2,1,0:T(8,128)(2,1)} %convert_bitcast_fusion.2), kind=kLoop, calls=%fused_computation.24 | loop fusion | flops 6291456 | bytes 12582912 | tf_op jit(solution)/shard_map/broadcast_in_dim | solution.py:118
  (28 shorter events, 9.3 us)
Async XLA Ops:
  0.0 42.3 %copy-start.1 = (s32[1,2]{1,0:T(1,128)S(1)}, s32[1,2]{1,0:T(1,128)}, u32[]{:S(2)}) copy-start(s32[1,2]{1,0:T(1,128)} %param.9) | copy-start | bytes 28
  0.0 7.1 %collective-permute-start = (f32[256,256]{1,0:T(8,128)}, f32[256,256]{1,0:T(8,128)S(1)}, u32[]{:S(2)}, u32[]{:S(2)}) collective-permute-start(f32[256,256]{1,0:T(8,128)} %param.7), channel_id=1, source_target_pairs={{1,0},{4,1},{5,4},{8,5},{9,8},{12,9},{13,12},{3,2},{6,3},{7,6},{10... | collective-permute-start | bytes 786440 | tf_op jit(solution)/shard_map/ppermute | solution.py:16
  2.1 11.7 %collective-permute-start.1 = (f32[256,256]{1,0:T(8,128)}, f32[256,256]{1,0:T(8,128)S(1)}, u32[]{:S(2)}, u32[]{:S(2)}) collective-permute-start(f32[256,256]{1,0:T(8,128)} %param.7), channel_id=1, source_target_pairs={{4,0},{5,1},{8,4},{9,5},{12,8},{13,9},{6,2},{7,3},{10,6},{11,7},{1... | collective-permute-start | bytes 786440 | tf_op jit(solution)/shard_map/ppermute | solution.py:16
  42.2 14.0 %collective-permute-start.2 = (bf16[128,8,2,128]{0,1,2,3:T(8,128)(2,1)S(1)}, bf16[128,8,2,128]{0,1,2,3:T(8,128)(2,1)S(1)}, u32[]{:S(2)}, u32[]{:S(2)}) collective-permute-start(bf16[128,8,2,128]{0,1,2,3:T(8,128)(2,1)S(1)} %bitcast.92), channel_id=1, source_target_pairs={{0,2},{2,0},{1,3},{3,1},{4,6},{6,4},{5,7},{7,5},{8,10},{10,8},{9,1... | collective-permute-start | bytes 1572872 | tf_op jit(solution)/shard_map/ppermute | solution.py:91
  59.2 34.0 %collective-permute-start.3 = (bf16[64,8,2,256]{3,1,2,0:T(8,128)(2,1)}, bf16[64,8,2,256]{3,1,2,0:T(8,128)(2,1)}, u32[]{:S(2)}, u32[]{:S(2)}) collective-permute-start(bf16[64,8,2,256]{3,1,2,0:T(8,128)(2,1)} %copy.41), channel_id=1, source_target_pairs={{4,0},{8,4},{12,8},{5,1},{9,5},{13,9},{6,2},{10,6},{14,10},{7,3},{... | collective-permute-start | bytes 1572872 | tf_op jit(solution)/shard_map/ppermute | solution.py:16
  63.0 55.8 %collective-permute-start.4 = (bf16[64,8,2,256]{3,1,2,0:T(8,128)(2,1)}, bf16[64,8,2,256]{3,1,2,0:T(8,128)(2,1)}, u32[]{:S(2)}, u32[]{:S(2)}) collective-permute-start(bf16[64,8,2,256]{3,1,2,0:T(8,128)(2,1)} %copy.41), channel_id=1, source_target_pairs={{8,0},{12,4},{9,1},{13,5},{10,2},{14,6},{11,3},{15,7},{24,16},{28,... | collective-permute-start | bytes 1572872 | tf_op jit(solution)/shard_map/ppermute | solution.py:16
  118.8 1.3 copy-start
